TPU v7x, 256 devices: a whole 4x4x8 slice. The times are simulated.
256 devices in a mesh: group: 8 (over y, core), dom: 32 (over z, x).
Axes of the slice: x: 4, y: 4, z: 8, core: 2. Of those that a mesh axis runs over, the one named last changes fastest.
Arguments:
- node_feats: bfloat16 [524288, 512], P(('group', 'dom')), may hold values from -36 to 36
- send_rows: int32 [256, 32, 32], P(('group', 'dom')), may hold values from 0 to 2047
- hub_rows: int32 [256, 8], P(('group', 'dom')), may hold values from 0 to 2047
- neighbours: int32 [524288, 16], P(('group', 'dom')), may hold values from 0 to 5119, as said below
- w_self: bfloat16 [512, 512], replicated, may hold values from -0.25 to 0.25
- w_neigh: bfloat16 [512, 512], replicated, may hold values from -0.25 to 0.25
- w_head: bfloat16 [512, 128], replicated, may hold values from -1.5 to 1.5
- s_first: bfloat16 [512, 512], replicated, may hold values from -0.25 to 0.25
- s_second: bfloat16 [512, 128], replicated, may hold values from -1.5 to 1.5
Outputs:
- teacher_hidden: bfloat16 [524288, 512], P(('group', 'dom'))
- grad_first: float32 [512, 512], replicated
- grad_second: float32 [512, 128], replicated
Inputs may be any that keep to these rules, and one draw needn't show every extreme that they name: `neighbours`: entries below 2048 are local rows; entries from 2048 to 3071 name halo rows, and from a given peer only its first rows, up to 32; the rest name hubs.
All inputs are finite; a program needn't handle non-finite values.
Results may differ from a plain program's by a relative error of at most 0.0025.
Values may be sent and summed in bfloat16 or wider, within the bound.
No kernel may reach another device: no remote copies, remote signals or barrier semaphores. Data moves between devices by JAX's collectives and lax.ppermute only.
A program may use at most 128 MiB of HBM per device.

v0:
```python
import jax
import jax.numpy as jnp
from jax import lax
from jax.sharding import PartitionSpec as P

DEG = 16
TEMPER = 2.0


def local_layer(feats, table, nbr, w_self, w_neigh, w_head, s_first, s_second, scale):
    rows = feats.shape[0]
    block = min(512, rows)

    def agg_block(index):
        picked = table[index].astype(jnp.float32)
        return (jnp.sum(picked, axis=1) / DEG).astype(jnp.bfloat16)

    agg = lax.map(agg_block, nbr.reshape(rows // block, block, DEG)).reshape(rows, feats.shape[1])
    pre = jnp.dot(feats, w_self, preferred_element_type=jnp.float32) + jnp.dot(
        agg, w_neigh, preferred_element_type=jnp.float32
    )
    hidden = jax.nn.relu(pre).astype(jnp.bfloat16)
    t_logits = jnp.dot(hidden, w_head, preferred_element_type=jnp.float32)
    s_pre = jnp.dot(feats, s_first, preferred_element_type=jnp.float32)
    s_hidden = jax.nn.relu(s_pre).astype(jnp.bfloat16)
    s_logits = jnp.dot(s_hidden, s_second, preferred_element_type=jnp.float32)
    p_teach = jax.nn.softmax(t_logits / TEMPER, axis=-1)
    p_stud = jax.nn.softmax(s_logits / TEMPER, axis=-1)
    delta = (TEMPER * (p_stud - p_teach) * scale).astype(jnp.bfloat16)
    g_second = jnp.dot(s_hidden.T, delta, preferred_element_type=jnp.float32)
    back = jnp.dot(delta, s_second.T, preferred_element_type=jnp.float32)
    back = jnp.where(s_pre > 0, back, 0.0).astype(jnp.bfloat16)
    g_first = jnp.dot(feats.T, back, preferred_element_type=jnp.float32)
    return (hidden, g_first, g_second)


def per_device(
    node_feats, send_rows, hub_rows, neighbours, w_self, w_neigh, w_head, s_first, s_second
):
    rows = node_feats.shape[0]
    width = node_feats.shape[1]
    outgoing = node_feats[send_rows[0]]
    received = lax.all_to_all(outgoing, "dom", split_axis=0, concat_axis=0, tiled=True)
    halo = received.reshape(-1, width)
    own_hubs = node_feats[hub_rows[0]]
    hubs = lax.all_gather(own_hubs, ("group", "dom"), axis=0, tiled=True)
    table = jnp.concatenate([node_feats, halo, hubs], axis=0)
    total_nodes = rows * lax.axis_size("group") * lax.axis_size("dom")
    scale = 1.0 / jnp.sqrt(jnp.float32(total_nodes))
    hidden, g_first, g_second = local_layer(
        node_feats, table, neighbours, w_self, w_neigh, w_head, s_first, s_second, scale
    )
    grad_first, grad_second = lax.psum((g_first, g_second), ("group", "dom"))
    return (hidden, grad_first, grad_second)


def solution(mesh):
    return jax.shard_map(
        per_device,
        mesh=mesh,
        in_specs=(
            P(("group", "dom"), None),
            P(("group", "dom"), None, None),
            P(("group", "dom"), None),
            P(("group", "dom"), None),
            P(),
            P(),
            P(),
            P(),
            P(),
        ),
        out_specs=(P(("group", "dom"), None), P(), P()),
        check_vma=False,
    )
```

profile of v0, /device:TPU:2, one launch (start us, length us, event | category | flops | bytes accessed | tf_op | source)
XLA Modules:
  0.0 601.0 jit_solution(7167910912744096948)
XLA Ops:
  7.9 3.0 gather_fusion.2
  11.8 7.1 %gather_fusion.1 = bf16[1024,512]{1,0:T(8,128)(2,1)} fusion(bf16[2048,512]{1,0:T(8,128)(2,1)} %param.11, s32[1024]{0:T(1024)S(1)} %broadcast_clamp_fusion.1), kind=kCustom, calls=%fused_computation.1 | custom fusion | bytes 2101248 | tf_op jit(solution)/shard_map/gather | solution.py:42
  18.9 11.7 %all-to-all-start = ((bf16[32,32,512]{2,1,0:T(8,128)(2,1)}), bf16[32,32,512]{2,1,0:T(8,128)(2,1)}, u32[]{:S(2)}, u32[]{:S(2)}) async-start(bf16[32,32,512]{2,1,0:T(8,128)(2,1)} %bitcast.43), calls=%async_computation | async-start | bytes 2097152 | tf_op jit(solution)/shard_map/all_to_all | solution.py:43
  33.2 1.9 copy-done.2
  35.1 1.8 fusion.12
  37.0 3.2 fusion.13
  40.2 18.6 %all-to-all-done = bf16[32,32,512]{2,1,0:T(8,128)(2,1)} async-done(((bf16[32,32,512]{2,1,0:T(8,128)(2,1)}), bf16[32,32,512]{2,1,0:T(8,128)(2,1)}, u32[]{:S(2)}, u32[]{:S(2)}) %all-to-all-start) | async-done | bytes 1048608 | tf_op jit(solution)/shard_map/all_to_all | solution.py:43
  58.8 61.9 %all-gather.3.cloned.1.call-done = bf16[2048,512]{1,0:T(8,128)(2,1)} async-done(((bf16[8,512]{1,0:T(8,128)(2,1)}), bf16[2048,512]{1,0:T(8,128)(2,1)}) %all-gather.3.cloned.1.call-update) | async-done | bytes 2097168 | tf_op jit(solution)/shard_map/all_gather | solution.py:46
  120.7 4.6 pad_maximum_fusion
  125.3 188.4 %while.10 = (s32[]{:T(128)}, bf16[4,512,512]{2,1,0:T(8,128)(2,1)}, s32[4,512,16]{2,1,0:T(8,128)}, bf16[5120,512]{1,0:T(8,128)(2,1)}, s32[]{:T(128)}) while((s32[]{:T(128)}, bf16[4,512,512]{2,1,0:T(8,128)(2,1)}, s32[4,512,16]{2,1,0:T(8,128)}, bf16[5120,512]{1,0:T(8,128)(2,1)}, s32[]{:T(128)}) %tuple.37), condition=%wide.region_2.3_spmd, body=%wide.region_0.2_spmd.sunk | while | flops 8683522 | bytes 28016716 | solution.py:18
  126.5 37.0 %gather_fusion = bf16[8192,512]{1,0:T(8,128)(2,1)} fusion(bf16[5120,512]{1,0:T(8,128)(2,1)} %get-tuple-element.90, s32[8192]{0:T(1024)S(1)} %broadcast_clamp_fusion.3), kind=kCustom, calls=%fused_computation.clone.1 | custom fusion | bytes 16809984 | tf_op jit(solution)/shard_map/while/body/eval_jaxpr/gather | solution.py:15
  163.5 8.0 %convert_reduce_fusion.2 = f32[512,512]{1,0:T(8,128)S(1)} fusion(bf16[8192,512]{1,0:T(8,128)(2,1)} %gather_fusion), kind=kLoop, calls=%fused_computation.3.clone.1 | loop fusion | flops 8126464 | bytes 9437184 | tf_op jit(solution)/shard_map/while/body/eval_jaxpr/reduce_sum | solution.py:16
  173.6 37.0 %gather_fusion = bf16[8192,512]{1,0:T(8,128)(2,1)} fusion(bf16[5120,512]{1,0:T(8,128)(2,1)} %get-tuple-element.90, s32[8192]{0:T(1024)S(1)} %broadcast_clamp_fusion.3), kind=kCustom, calls=%fused_computation.clone.1 | custom fusion | bytes 16809984 | tf_op jit(solution)/shard_map/while/body/eval_jaxpr/gather | solution.py:15
  210.6 8.0 %convert_reduce_fusion.2 = f32[512,512]{1,0:T(8,128)S(1)} fusion(bf16[8192,512]{1,0:T(8,128)(2,1)} %gather_fusion), kind=kLoop, calls=%fused_computation.3.clone.1 | loop fusion | flops 8126464 | bytes 9437184 | tf_op jit(solution)/shard_map/while/body/eval_jaxpr/reduce_sum | solution.py:16
  220.7 37.0 %gather_fusion = bf16[8192,512]{1,0:T(8,128)(2,1)} fusion(bf16[5120,512]{1,0:T(8,128)(2,1)} %get-tuple-element.90, s32[8192]{0:T(1024)S(1)} %broadcast_clamp_fusion.3), kind=kCustom, calls=%fused_computation.clone.1 | custom fusion | bytes 16809984 | tf_op jit(solution)/shard_map/while/body/eval_jaxpr/gather | solution.py:15
  257.7 8.0 %convert_reduce_fusion.2 = f32[512,512]{1,0:T(8,128)S(1)} fusion(bf16[8192,512]{1,0:T(8,128)(2,1)} %gather_fusion), kind=kLoop, calls=%fused_computation.3.clone.1 | loop fusion | flops 8126464 | bytes 9437184 | tf_op jit(solution)/shard_map/while/body/eval_jaxpr/reduce_sum | solution.py:16
  267.8 37.0 %gather_fusion = bf16[8192,512]{1,0:T(8,128)(2,1)} fusion(bf16[5120,512]{1,0:T(8,128)(2,1)} %get-tuple-element.90, s32[8192]{0:T(1024)S(1)} %broadcast_clamp_fusion.3), kind=kCustom, calls=%fused_computation.clone.1 | custom fusion | bytes 16809984 | tf_op jit(solution)/shard_map/while/body/eval_jaxpr/gather | solution.py:15
  304.8 8.0 %convert_reduce_fusion.2 = f32[512,512]{1,0:T(8,128)S(1)} fusion(bf16[8192,512]{1,0:T(8,128)(2,1)} %gather_fusion), kind=kLoop, calls=%fused_computation.3.clone.1 | loop fusion | flops 8126464 | bytes 9437184 | tf_op jit(solution)/shard_map/while/body/eval_jaxpr/reduce_sum | solution.py:16
  313.7 4.2 maximum_convert_fusion.1
  321.8 1.6 fusion.6
  323.4 6.0 %fusion.3 = f32[512,512]{0,1:T(8,128)} fusion(bf16[2048,512]{1,0:T(8,128)(2,1)S(1)} %copy-done.1, f32[2048,512]{1,0:T(8,128)} %copy-done.2, bf16[512,128]{1,0:T(8,128)(2,1)S(1)} %copy-done.12, f32[2048,128]{0,1:T(8,128)} %get-tuple-element.49, f32[2048,128]{0,1:T(8,128)} %copy-done.5, f32[2048]{0:T(1024)S(1)} %get-tuple-element.51, ...), kind=kOutput, calls=%fused_computation.16 | convolution fusion | flops 1347158016 | bytes 9601024 | tf_op jit(solution)/shard_map/dot_general | solution.py:33
  329.4 260.5 %all-reduce.3.cloned.1.call-done = (f32[512,512]{0,1:T(8,128)}, f32[512,128]{1,0:T(8,128)}) async-done(((f32[512,512]{0,1:T(8,128)}, f32[512,128]{1,0:T(8,128)}), (f32[512,512]{0,1:T(8,128)}, f32[512,128]{1,0:T(8,128)})) %all-reduce.3.cloned.1.call-update) | async-done | bytes 1310736 | tf_op jit(solution)/shard_map/psum | solution.py:53
  589.9 2.5 copy.14
  592.5 1.7 copy.27
  (55 shorter events, 16.3 us)
Async XLA Ops:
  7.2 24.8 %copy-start = (bf16[512,512]{1,0:T(8,128)(2,1)S(1)}, bf16[512,512]{1,0:T(8,128)(2,1)}, u32[]{:S(2)}) copy-start(bf16[512,512]{1,0:T(8,128)(2,1)} %param.18) | copy-start | bytes 1572868
  7.2 113.5 %all-gather.3.cloned.1.call-start = ((), (), s32[]{:S(2)}) async-start(), calls=%async_computation.1 | async-start | bytes 2105344 | tf_op jit(solution)/shard_map/all_gather | solution.py:46
  11.8 18.8 %copy-start.9 = (s32[2048,16]{0,1:T(8,128)S(1)}, s32[2048,16]{0,1:T(8,128)}, u32[]{:S(2)}) copy-start(s32[2048,16]{0,1:T(8,128)} %param.14) | copy-start | bytes 393220
  11.8 20.2 %copy-start.1 = (bf16[2048,512]{1,0:T(8,128)(2,1)S(1)}, bf16[2048,512]{1,0:T(8,128)(2,1)}, u32[]{:S(2)}) copy-start(bf16[2048,512]{1,0:T(8,128)(2,1)} %param.11) | copy-start | bytes 6291460
  18.9 39.9 %all-to-all-start = ((bf16[32,32,512]{2,1,0:T(8,128)(2,1)}), bf16[32,32,512]{2,1,0:T(8,128)(2,1)}, u32[]{:S(2)}, u32[]{:S(2)}) async-start(bf16[32,32,512]{2,1,0:T(8,128)(2,1)} %bitcast.43), calls=%async_computation | async-start | bytes 2097152 | tf_op jit(solution)/shard_map/all_to_all | solution.py:43
  30.6 559.4 %all-reduce.3.cloned.1.call-start = ((), (), s32[]{:S(2)}) async-start(), calls=%async_computation.2 | async-start | bytes 2621440 | tf_op jit(solution)/shard_map/psum | solution.py:53
  32.0 3.2 copy-start.11
  33.2 1.9 copy-start.2
  35.1 1.8 copy-start.7
  125.3 188.4 %copy-start.8 = (bf16[512,512]{1,0:T(8,128)(2,1)S(1)}, bf16[512,512]{1,0:T(8,128)(2,1)}, u32[]{:S(2)}) copy-start(bf16[512,512]{1,0:T(8,128)(2,1)} %param.16) | copy-start | bytes 1572868
  313.7 5.5 copy-start.10
  313.7 6.3 %copy-start.6 = (f32[2048,128]{0,1:T(8,128)S(1)}, f32[2048,128]{0,1:T(8,128)}, u32[]{:S(2)}) copy-start(f32[2048,128]{0,1:T(8,128)} %get-tuple-element.49) | copy-start | bytes 3145732
  317.9 1.3 copy-start.4
  319.2 2.6 copy-start.3
  320.1 1.0 copy-start.5
  321.8 1.6 copy-start.12
Sparse Core Ops, SparseCore 0:
  12.3 108.3 all-gather.2
  329.5 260.3 all-reduce.2
where the time goes:
time: 602 us; the launch traced here: 601 us
  waiting for transfers between devices  341 us (57%)
  local copies, waits for them, and re-layouts  169 us (28%)
  other arithmetic  46.2 us (8%)
  matrix products  18.9 us (3%)
  between operations  14.1 us (2%)
  starting transfers between devices  11.7 us (2%)
    psum x1, waiting for transfers between devices, per_device(): grad_first, grad_second = lax.psum((g_first, g_second), ('group', 'dom'))  261 us
    gather x4, local copies, waits for them, and re-layouts, agg_block(): picked = table[index].astype(jnp.float32)  148 us
    all_gather x1, waiting for transfers between devices, per_device(): hubs = lax.all_gather(own_hubs, ('group', 'dom'), axis=0, tiled=True)  61.9 us
    reduce_sum x4, other arithmetic, agg_block(): return (jnp.sum(picked, axis=1) / DEG).astype(jnp.bfloat16)  32.1 us
    all_to_all x1, waiting for transfers between devices, per_device(): lax.all_to_all(outgoing, 'dom', split_axis=0, concat_axis=0, tiled=True)  18.6 us
  transfers between devices with their start and end apart: 3, of which 3 were waited for; matrix products, arithmetic and copies ran while one was open for 3% of the time, Pallas kernels for 0%

commit v1 on v0

--- a/solution.py
+++ b/solution.py
@@ -50,7 +50,7 @@
     hidden, g_first, g_second = local_layer(
         node_feats, table, neighbours, w_self, w_neigh, w_head, s_first, s_second, scale
     )
-    grad_first, grad_second = lax.psum((g_first, g_second), ("group", "dom"))
+    grad_first, grad_second = lax.psum(lax.psum((g_first, g_second), "dom"), "group")
     return (hidden, grad_first, grad_second)
 
 

time: 602 us -> 560 us (0.930)
  waiting for transfers between devices: 341 us -> 299 us
    psum x1 -> x2, waiting for transfers between devices: 261 us -> 219 us  [the longest x1 150 us: per_device(): lax.psum((g_first, g_second), 'dom')]
  transfers between devices with their start and end apart: 3 -> 4, of which waited for: 3 -> 4; matrix products, arithmetic and copies ran while one was open for 3% -> 3% of each run, Pallas kernels for 0% -> 0%
where the time goes in v1:
time: 560 us; the launch traced here: 559 us
  waiting for transfers between devices  299 us (53%)
  local copies, waits for them, and re-layouts  169 us (30%)
  other arithmetic  46.2 us (8%)
  matrix products  18.9 us (3%)
  between operations  13.8 us (2%)
  starting transfers between devices  11.8 us (2%)
    psum x1, waiting for transfers between devices, per_device(): lax.psum((g_first, g_second), 'dom')  150 us
    gather x4, local copies, waits for them, and re-layouts, agg_block(): picked = table[index].astype(jnp.float32)  148 us
    psum x1, waiting for transfers between devices, per_device(): lax.psum(lax.psum((g_first, g_second), 'dom'), 'group')  69.4 us
    all_gather x1, waiting for transfers between devices, per_device(): hubs = lax.all_gather(own_hubs, ('group', 'dom'), axis=0, tiled=True)  61.9 us
    reduce_sum x4, other arithmetic, agg_block(): return (jnp.sum(picked, axis=1) / DEG).astype(jnp.bfloat16)  32.1 us
    all_to_all x1, waiting for transfers between devices, per_device(): lax.all_to_all(outgoing, 'dom', split_axis=0, concat_axis=0, tiled=True)  18.6 us
    all_to_all x1, starting transfers between devices, per_device(): lax.all_to_all(outgoing, 'dom', split_axis=0, concat_axis=0, tiled=True)  11.7 us
  transfers between devices with their start and end apart: 4, of which 4 were waited for; matrix products, arithmetic and copies ran while one was open for 3% of the time, Pallas kernels for 0%

profile of v1, /device:TPU:2, one launch (start us, length us, event | category | flops | bytes accessed | tf_op | source)
XLA Modules:
  0.0 559.0 jit_solution(3197817706515174730)
XLA Ops:
  7.9 3.0 gather_fusion.2
  11.8 7.1 %gather_fusion.1 = bf16[1024,512]{1,0:T(8,128)(2,1)} fusion(bf16[2048,512]{1,0:T(8,128)(2,1)} %param.11, s32[1024]{0:T(1024)S(1)} %broadcast_clamp_fusion.1), kind=kCustom, calls=%fused_computation.1 | custom fusion | bytes 2101248 | tf_op jit(solution)/shard_map/gather | solution.py:42
  18.9 11.7 %all-to-all-start = ((bf16[32,32,512]{2,1,0:T(8,128)(2,1)}), bf16[32,32,512]{2,1,0:T(8,128)(2,1)}, u32[]{:S(2)}, u32[]{:S(2)}) async-start(bf16[32,32,512]{2,1,0:T(8,128)(2,1)} %bitcast.43), calls=%async_computation | async-start | bytes 2097152 | tf_op jit(solution)/shard_map/all_to_all | solution.py:43
  33.2 1.9 copy-done.2
  35.2 1.8 fusion.12
  37.0 3.2 fusion.13
  40.2 18.6 %all-to-all-done = bf16[32,32,512]{2,1,0:T(8,128)(2,1)} async-done(((bf16[32,32,512]{2,1,0:T(8,128)(2,1)}), bf16[32,32,512]{2,1,0:T(8,128)(2,1)}, u32[]{:S(2)}, u32[]{:S(2)}) %all-to-all-start) | async-done | bytes 1048608 | tf_op jit(solution)/shard_map/all_to_all | solution.py:43
  58.8 61.9 %all-gather.3.cloned.1.call-done = bf16[2048,512]{1,0:T(8,128)(2,1)} async-done(((bf16[8,512]{1,0:T(8,128)(2,1)}), bf16[2048,512]{1,0:T(8,128)(2,1)}) %all-gather.3.cloned.1.call-update) | async-done | bytes 2097168 | tf_op jit(solution)/shard_map/all_gather | solution.py:46
  120.7 4.6 pad_maximum_fusion
  125.3 188.2 %while.10 = (s32[]{:T(128)}, bf16[4,512,512]{2,1,0:T(8,128)(2,1)}, s32[4,512,16]{2,1,0:T(8,128)}, bf16[5120,512]{1,0:T(8,128)(2,1)}, s32[]{:T(128)}) while((s32[]{:T(128)}, bf16[4,512,512]{2,1,0:T(8,128)(2,1)}, s32[4,512,16]{2,1,0:T(8,128)}, bf16[5120,512]{1,0:T(8,128)(2,1)}, s32[]{:T(128)}) %tuple.40), condition=%wide.region_2.3_spmd, body=%wide.region_0.2_spmd.sunk | while | flops 8683522 | bytes 28016716 | solution.py:18
  126.5 37.0 %gather_fusion = bf16[8192,512]{1,0:T(8,128)(2,1)} fusion(bf16[5120,512]{1,0:T(8,128)(2,1)} %get-tuple-element.92, s32[8192]{0:T(1024)S(1)} %broadcast_clamp_fusion.3), kind=kCustom, calls=%fused_computation.clone.1 | custom fusion | bytes 16809984 | tf_op jit(solution)/shard_map/while/body/eval_jaxpr/gather | solution.py:15
  163.5 8.0 %convert_reduce_fusion.2 = f32[512,512]{1,0:T(8,128)S(1)} fusion(bf16[8192,512]{1,0:T(8,128)(2,1)} %gather_fusion), kind=kLoop, calls=%fused_computation.3.clone.1 | loop fusion | flops 8126464 | bytes 9437184 | tf_op jit(solution)/shard_map/while/body/eval_jaxpr/reduce_sum | solution.py:16
  173.6 37.0 %gather_fusion = bf16[8192,512]{1,0:T(8,128)(2,1)} fusion(bf16[5120,512]{1,0:T(8,128)(2,1)} %get-tuple-element.92, s32[8192]{0:T(1024)S(1)} %broadcast_clamp_fusion.3), kind=kCustom, calls=%fused_computation.clone.1 | custom fusion | bytes 16809984 | tf_op jit(solution)/shard_map/while/body/eval_jaxpr/gather | solution.py:15
  210.5 8.0 %convert_reduce_fusion.2 = f32[512,512]{1,0:T(8,128)S(1)} fusion(bf16[8192,512]{1,0:T(8,128)(2,1)} %gather_fusion), kind=kLoop, calls=%fused_computation.3.clone.1 | loop fusion | flops 8126464 | bytes 9437184 | tf_op jit(solution)/shard_map/while/body/eval_jaxpr/reduce_sum | solution.py:16
  220.6 37.0 %gather_fusion = bf16[8192,512]{1,0:T(8,128)(2,1)} fusion(bf16[5120,512]{1,0:T(8,128)(2,1)} %get-tuple-element.92, s32[8192]{0:T(1024)S(1)} %broadcast_clamp_fusion.3), kind=kCustom, calls=%fused_computation.clone.1 | custom fusion | bytes 16809984 | tf_op jit(solution)/shard_map/while/body/eval_jaxpr/gather | solution.py:15
  257.6 8.0 %convert_reduce_fusion.2 = f32[512,512]{1,0:T(8,128)S(1)} fusion(bf16[8192,512]{1,0:T(8,128)(2,1)} %gather_fusion), kind=kLoop, calls=%fused_computation.3.clone.1 | loop fusion | flops 8126464 | bytes 9437184 | tf_op jit(solution)/shard_map/while/body/eval_jaxpr/reduce_sum | solution.py:16
  267.7 37.0 %gather_fusion = bf16[8192,512]{1,0:T(8,128)(2,1)} fusion(bf16[5120,512]{1,0:T(8,128)(2,1)} %get-tuple-element.92, s32[8192]{0:T(1024)S(1)} %broadcast_clamp_fusion.3), kind=kCustom, calls=%fused_computation.clone.1 | custom fusion | bytes 16809984 | tf_op jit(solution)/shard_map/while/body/eval_jaxpr/gather | solution.py:15
  304.6 8.0 %convert_reduce_fusion.2 = f32[512,512]{1,0:T(8,128)S(1)} fusion(bf16[8192,512]{1,0:T(8,128)(2,1)} %gather_fusion), kind=kLoop, calls=%fused_computation.3.clone.1 | loop fusion | flops 8126464 | bytes 9437184 | tf_op jit(solution)/shard_map/while/body/eval_jaxpr/reduce_sum | solution.py:16
  313.6 4.2 maximum_convert_fusion.1
  323.2 6.0 %fusion.3 = f32[512,512]{0,1:T(8,128)} fusion(bf16[2048,512]{1,0:T(8,128)(2,1)S(1)} %copy-done.1, f32[2048,512]{1,0:T(8,128)} %copy-done.2, bf16[512,128]{1,0:T(8,128)(2,1)S(1)} %copy-done.12, f32[2048,128]{0,1:T(8,128)} %get-tuple-element.51, f32[2048,128]{0,1:T(8,128)} %copy-done.5, f32[2048]{0:T(1024)S(1)} %get-tuple-element.53, ...), kind=kOutput, calls=%fused_computation.16 | convolution fusion | flops 1347158016 | bytes 9601024 | tf_op jit(solution)/shard_map/dot_general | solution.py:33
  329.3 149.5 %all-reduce.5.cloned.1.call-done = (f32[512,512]{0,1:T(8,128)}, f32[512,128]{1,0:T(8,128)}) async-done(((f32[512,512]{0,1:T(8,128)}, f32[512,128]{1,0:T(8,128)}), (f32[512,512]{0,1:T(8,128)}, f32[512,128]{1,0:T(8,128)})) %all-reduce.5.cloned.1.call-update) | async-done | bytes 1310736 | tf_op jit(solution)/shard_map/psum | solution.py:53
  478.8 69.4 %all-reduce.7.cloned.1.call-done = (f32[512,512]{0,1:T(8,128)}, f32[512,128]{1,0:T(8,128)}) async-done(((f32[512,512]{0,1:T(8,128)}, f32[512,128]{1,0:T(8,128)}), (f32[512,512]{0,1:T(8,128)}, f32[512,128]{1,0:T(8,128)})) %all-reduce.7.cloned.1.call-update) | async-done | bytes 1310736 | tf_op jit(solution)/shard_map/psum | solution.py:53
  548.3 2.5 copy.14
  550.8 1.7 copy.29
  (58 shorter events, 17.9 us)
Async XLA Ops:
  7.2 24.8 %copy-start = (bf16[512,512]{1,0:T(8,128)(2,1)S(1)}, bf16[512,512]{1,0:T(8,128)(2,1)}, u32[]{:S(2)}) copy-start(bf16[512,512]{1,0:T(8,128)(2,1)} %param.18) | copy-start | bytes 1572868
  7.2 113.6 %all-gather.3.cloned.1.call-start = ((), (), s32[]{:S(2)}) async-start(), calls=%async_computation.1 | async-start | bytes 2105344 | tf_op jit(solution)/shard_map/all_gather | solution.py:46
  11.8 18.9 %copy-start.9 = (s32[2048,16]{0,1:T(8,128)S(1)}, s32[2048,16]{0,1:T(8,128)}, u32[]{:S(2)}) copy-start(s32[2048,16]{0,1:T(8,128)} %param.14) | copy-start | bytes 393220
  11.8 20.2 %copy-start.1 = (bf16[2048,512]{1,0:T(8,128)(2,1)S(1)}, bf16[2048,512]{1,0:T(8,128)(2,1)}, u32[]{:S(2)}) copy-start(bf16[2048,512]{1,0:T(8,128)(2,1)} %param.11) | copy-start | bytes 6291460
  18.9 39.9 %all-to-all-start = ((bf16[32,32,512]{2,1,0:T(8,128)(2,1)}), bf16[32,32,512]{2,1,0:T(8,128)(2,1)}, u32[]{:S(2)}, u32[]{:S(2)}) async-start(bf16[32,32,512]{2,1,0:T(8,128)(2,1)} %bitcast.43), calls=%async_computation | async-start | bytes 2097152 | tf_op jit(solution)/shard_map/all_to_all | solution.py:43
  30.6 448.2 %all-reduce.5.cloned.1.call-start = ((), (), s32[]{:S(2)}) async-start(), calls=%async_computation.2 | async-start | bytes 2621440 | tf_op jit(solution)/shard_map/psum | solution.py:53
  32.0 3.2 copy-start.11
  33.2 1.9 copy-start.2
  35.2 1.8 copy-start.7
  125.3 188.2 %copy-start.8 = (bf16[512,512]{1,0:T(8,128)(2,1)S(1)}, bf16[512,512]{1,0:T(8,128)(2,1)}, u32[]{:S(2)}) copy-start(bf16[512,512]{1,0:T(8,128)(2,1)} %param.16) | copy-start | bytes 1572868
  313.6 5.5 copy-start.10
  313.6 6.3 %copy-start.6 = (f32[2048,128]{0,1:T(8,128)S(1)}, f32[2048,128]{0,1:T(8,128)}, u32[]{:S(2)}) copy-start(f32[2048,128]{0,1:T(8,128)} %get-tuple-element.51) | copy-start | bytes 3145732
  317.8 1.3 copy-start.4
  319.1 2.6 copy-start.3
  319.9 1.0 copy-start.5
  321.6 1.6 copy-start.12
  329.3 219.0 %all-reduce.7.cloned.1.call-start = ((), (), s32[]{:S(2)}) async-start(), calls=%async_computation.3 | async-start | bytes 2621440 | tf_op jit(solution)/shard_map/psum | solution.py:53
Sparse Core Ops, SparseCore 0:
  12.3 108.4 all-gather.2
  329.4 149.3 all-reduce.4
  481.3 66.9 all-reduce.6
